TPU v7x, 32 devices: a whole 2x2x4 slice. The times are simulated.
32 devices in a mesh: row: 4 (over z), col: 8 (over y, x, core).
Axes of the slice: x: 2, y: 2, z: 4, core: 2. Of those that a mesh axis runs over, the one named last changes fastest.
Arguments:
- root_factor: float32 [2, 4, 2560, 20480], P(None, 'row', None, 'col'), may hold values from -0.0390625 to 0.0390625
- root_rhs: float32 [20480, 64], P('col'), may hold values from -6 to 6
- child_factor: float32 [8, 4096, 4096], P('col', 'row'), may hold values from -0.09375 to 0.09375
- child_rhs: float32 [8, 4096, 64], P('col', 'row'), may hold values from -6 to 6
- child_map: int32 [8, 4096], P('col'), may hold values from 0 to 20479, as said below
Outputs:
- root_solution: float32 [20480, 64], P('col')
- child_solution: float32 [8, 4096, 64], P('col', 'row')
Inputs may be any that keep to these rules, and one draw needn't show every extreme that they name: Each row of child_map is strictly increasing; its entries at positions j * 512 to (j + 1) * 512 - 1 lie in root rows j * 2560 to (j + 1) * 2560 - 1.
All inputs are finite; a program needn't handle non-finite values.
Results may differ from a plain program's by a relative error of at most 0.0001.
Values sent between devices are 32-bit elements; how exact they have to be, the bound alone decides.
No kernel may reach another device: no remote copies, remote signals or barrier semaphores. Data moves between devices by JAX's collectives and lax.ppermute only.
A program may use at most 128 MiB of HBM per device.

v0:
```python
import jax
import jax.numpy as jnp
from jax import lax
from jax.sharding import PartitionSpec as P


def spread(block, axis, source):
    block = jnp.where(lax.axis_index(axis) == source, block, jnp.zeros_like(block))
    return lax.psum(block, axis)


def spread_panel(partial_value, owner_row):
    summed = lax.psum(partial_value, "col")
    return spread(summed, "row", owner_row)


def solve_panel(panel_id, solved, blocks, root_rhs, global_rows):
    row_count = lax.axis_size("row")
    block_slot = panel_id // row_count
    owner_row = panel_id % row_count
    panel_rows = lax.dynamic_index_in_dim(blocks, block_slot, 0, keepdims=False)
    partial_value = jnp.dot(
        panel_rows, solved, precision=lax.Precision.HIGHEST, preferred_element_type=jnp.float32
    )
    summed = spread_panel(partial_value, owner_row)
    panel_size = panel_rows.shape[0]
    offset = global_rows - panel_id * panel_size
    inside = (offset >= 0) & (offset < panel_size)
    picked = jnp.take(summed, jnp.clip(offset, 0, panel_size - 1), axis=0)
    return jnp.where(inside[:, None], root_rhs - picked, solved)


def body(root_factor, root_rhs, child_factor, child_rhs, child_map):
    blocks = root_factor[:, 0]
    own_rows = blocks.shape[2]
    panel_count = blocks.shape[0] * lax.axis_size("row")
    col_id = lax.axis_index("col")
    global_rows = col_id * own_rows + jnp.arange(own_rows, dtype=jnp.int32)

    def advance(turn, solved):
        upper = panel_count - 1 - 2 * turn
        solved = solve_panel(upper, solved, blocks, root_rhs, global_rows)
        return solve_panel(upper - 1, solved, blocks, root_rhs, global_rows)

    solved = lax.fori_loop(0, panel_count // 2, advance, jnp.zeros(root_rhs.shape, jnp.float32))
    child_block = child_factor[0]
    row_map = child_map[0]
    col_count = lax.axis_size("col")
    per_owner = row_map.shape[0] // col_count
    wanted = row_map.reshape(col_count, per_owner)
    asked = lax.all_to_all(wanted, "col", split_axis=0, concat_axis=0, tiled=True)
    served = jnp.take(solved, asked - col_id * own_rows, axis=0)
    parent_rows = lax.all_to_all(served, "col", split_axis=0, concat_axis=0, tiled=True)
    coupled = jnp.dot(
        child_block,
        parent_rows.reshape(row_map.shape[0], solved.shape[1]),
        precision=lax.Precision.HIGHEST,
        preferred_element_type=jnp.float32,
    )
    child_solution = child_rhs - coupled[None]
    return (solved, child_solution)


def solution(mesh):
    return jax.shard_map(
        body,
        mesh=mesh,
        in_specs=(
            P(None, "row", None, "col"),
            P("col", None),
            P("col", "row", None),
            P("col", "row", None),
            P("col", None),
        ),
        out_specs=(P("col", None), P("col", "row", None)),
        check_vma=False,
    )
```

profile of v0, /device:TPU:0, one launch (start us, length us, event | category | flops | bytes accessed | tf_op | source)
XLA Modules:
  0.0 1184.0 jit_solution(4137197244036961348)
XLA Ops:
  7.2 5.2 all-to-all-start
  12.4 2.6 copy.18
  15.0 2.2 all-to-all-done
  17.2 1106.1 %while.19 = (s32[]{:T(128)}, f32[2560,64]{1,0:T(8,128)S(1)}, f32[2,2560,2560]{2,1,0:T(8,128)}, f32[2560,64]{1,0:T(8,128)}, s32[]{:T(128)}, /*index=5*/s32[]{:T(1...) while((s32[]{:T(128)}, f32[2560,64]{1,0:T(8,128)S(1)}, ...), condition=%wide.region_5.7_spmd.clone, body=%wide.region_0.6_spmd.clone.sunk | while | flops 10069377024 | bytes 84653952 | solution.py:45
  17.3 29.3 %fusion.49 = f32[2560,64]{0,1:T(8,128)} fusion(f32[2,2560,2560]{2,1,0:T(8,128)} %get-tuple-element.329, s32[]{:T(128)S(6)} %select_n.295, f32[2560,64]{1,0:T(8,128)S(1)} %get-tuple-element.313, pred[]{:T(512)S(6)} %compare.37), kind=kOutput, calls=%fused_computation.4.clone.1 | convolution fusion | flops 5033328640 | bytes 27525124 | tf_op jit(solution)/shard_map/while/body/eval_jaxpr/dot_general | solution.py:22
  46.7 54.9 %all-reduce.5.cloned.1.call-done = f32[2560,64]{0,1:T(8,128)} async-done(((f32[2560,64]{0,1:T(8,128)}), f32[2560,64]{0,1:T(8,128)}) %all-reduce.5.cloned.1.call-update) | async-done | bytes 655376 | tf_op jit(solution)/shard_map/while/body/eval_jaxpr/psum | solution.py:13
  102.6 41.8 %all-reduce.7.cloned.1.call-done = f32[2560,64]{0,1:T(8,128)} async-done(((f32[2560,64]{0,1:T(8,128)}), f32[2560,64]{0,1:T(8,128)}) %all-reduce.7.cloned.1.call-update) | async-done | bytes 655376 | tf_op jit(solution)/shard_map/while/body/eval_jaxpr/psum | solution.py:9
  145.9 5.6 gather_fusion
  151.5 31.5 %fusion.51 = f32[2560,64]{0,1:T(8,128)} fusion(f32[2,2560,2560]{2,1,0:T(8,128)} %get-tuple-element.329, s32[]{:T(128)S(6)} %select_n.293, f32[2560,64]{1,0:T(8,128)} %get-tuple-element.330, f32[2560,64]{1,0:T(8,128)} %gather_fusion, f32[2560,64]{1,0:T(8,128)S(1)} %get-tuple-element.313, pred[2560]{0:T(1024)(128)(4,1)S(1)} %get-tuple-element.293, ...), kind=kOutput, calls=%fused_computation.6.clone.1 | convolution fusion | flops 5033820160 | bytes 30151684 | tf_op jit(solution)/shard_map/while/body/eval_jaxpr/dot_general | solution.py:22
  183.1 54.8 %all-reduce.9.cloned.1.call-done = f32[2560,64]{0,1:T(8,128)} async-done(((f32[2560,64]{0,1:T(8,128)}), f32[2560,64]{0,1:T(8,128)}) %all-reduce.9.cloned.1.call-update) | async-done | bytes 655376 | tf_op jit(solution)/shard_map/while/body/eval_jaxpr/psum | solution.py:13
  238.9 41.7 %all-reduce.11.cloned.1.call-done = f32[2560,64]{0,1:T(8,128)} async-done(((f32[2560,64]{0,1:T(8,128)}), f32[2560,64]{0,1:T(8,128)}) %all-reduce.11.cloned.1.call-update) | async-done | bytes 655376 | tf_op jit(solution)/shard_map/while/body/eval_jaxpr/psum | solution.py:9
  282.1 5.6 gather_fusion.1
  287.8 6.0 fusion.53
  293.9 29.3 %fusion.49 = f32[2560,64]{0,1:T(8,128)} fusion(f32[2,2560,2560]{2,1,0:T(8,128)} %get-tuple-element.329, s32[]{:T(128)S(6)} %select_n.295, f32[2560,64]{1,0:T(8,128)S(1)} %get-tuple-element.313, pred[]{:T(512)S(6)} %compare.37), kind=kOutput, calls=%fused_computation.4.clone.1 | convolution fusion | flops 5033328640 | bytes 27525124 | tf_op jit(solution)/shard_map/while/body/eval_jaxpr/dot_general | solution.py:22
  323.3 54.9 %all-reduce.5.cloned.1.call-done = f32[2560,64]{0,1:T(8,128)} async-done(((f32[2560,64]{0,1:T(8,128)}), f32[2560,64]{0,1:T(8,128)}) %all-reduce.5.cloned.1.call-update) | async-done | bytes 655376 | tf_op jit(solution)/shard_map/while/body/eval_jaxpr/psum | solution.py:13
  379.2 41.7 %all-reduce.7.cloned.1.call-done = f32[2560,64]{0,1:T(8,128)} async-done(((f32[2560,64]{0,1:T(8,128)}), f32[2560,64]{0,1:T(8,128)}) %all-reduce.7.cloned.1.call-update) | async-done | bytes 655376 | tf_op jit(solution)/shard_map/while/body/eval_jaxpr/psum | solution.py:9
  422.3 5.6 gather_fusion
  427.9 31.5 %fusion.51 = f32[2560,64]{0,1:T(8,128)} fusion(f32[2,2560,2560]{2,1,0:T(8,128)} %get-tuple-element.329, s32[]{:T(128)S(6)} %select_n.293, f32[2560,64]{1,0:T(8,128)} %get-tuple-element.330, f32[2560,64]{1,0:T(8,128)} %gather_fusion, f32[2560,64]{1,0:T(8,128)S(1)} %get-tuple-element.313, pred[2560]{0:T(1024)(128)(4,1)S(1)} %get-tuple-element.293, ...), kind=kOutput, calls=%fused_computation.6.clone.1 | convolution fusion | flops 5033820160 | bytes 30151684 | tf_op jit(solution)/shard_map/while/body/eval_jaxpr/dot_general | solution.py:22
  459.6 54.8 %all-reduce.9.cloned.1.call-done = f32[2560,64]{0,1:T(8,128)} async-done(((f32[2560,64]{0,1:T(8,128)}), f32[2560,64]{0,1:T(8,128)}) %all-reduce.9.cloned.1.call-update) | async-done | bytes 655376 | tf_op jit(solution)/shard_map/while/body/eval_jaxpr/psum | solution.py:13
  514.4 2.0 broadcast_select_fusion.6
  516.5 40.8 %all-reduce.11.cloned.1.call-done = f32[2560,64]{0,1:T(8,128)} async-done(((f32[2560,64]{0,1:T(8,128)}), f32[2560,64]{0,1:T(8,128)}) %all-reduce.11.cloned.1.call-update) | async-done | bytes 655376 | tf_op jit(solution)/shard_map/while/body/eval_jaxpr/psum | solution.py:9
  558.7 5.6 gather_fusion.1
  564.3 6.0 fusion.53
  570.5 29.3 %fusion.49 = f32[2560,64]{0,1:T(8,128)} fusion(f32[2,2560,2560]{2,1,0:T(8,128)} %get-tuple-element.329, s32[]{:T(128)S(6)} %select_n.295, f32[2560,64]{1,0:T(8,128)S(1)} %get-tuple-element.313, pred[]{:T(512)S(6)} %compare.37), kind=kOutput, calls=%fused_computation.4.clone.1 | convolution fusion | flops 5033328640 | bytes 27525124 | tf_op jit(solution)/shard_map/while/body/eval_jaxpr/dot_general | solution.py:22
  599.9 54.9 %all-reduce.5.cloned.1.call-done = f32[2560,64]{0,1:T(8,128)} async-done(((f32[2560,64]{0,1:T(8,128)}), f32[2560,64]{0,1:T(8,128)}) %all-reduce.5.cloned.1.call-update) | async-done | bytes 655376 | tf_op jit(solution)/shard_map/while/body/eval_jaxpr/psum | solution.py:13
  655.8 41.6 %all-reduce.7.cloned.1.call-done = f32[2560,64]{0,1:T(8,128)} async-done(((f32[2560,64]{0,1:T(8,128)}), f32[2560,64]{0,1:T(8,128)}) %all-reduce.7.cloned.1.call-update) | async-done | bytes 655376 | tf_op jit(solution)/shard_map/while/body/eval_jaxpr/psum | solution.py:9
  698.9 5.6 gather_fusion
  704.5 31.5 %fusion.51 = f32[2560,64]{0,1:T(8,128)} fusion(f32[2,2560,2560]{2,1,0:T(8,128)} %get-tuple-element.329, s32[]{:T(128)S(6)} %select_n.293, f32[2560,64]{1,0:T(8,128)} %get-tuple-element.330, f32[2560,64]{1,0:T(8,128)} %gather_fusion, f32[2560,64]{1,0:T(8,128)S(1)} %get-tuple-element.313, pred[2560]{0:T(1024)(128)(4,1)S(1)} %get-tuple-element.293, ...), kind=kOutput, calls=%fused_computation.6.clone.1 | convolution fusion | flops 5033820160 | bytes 30151684 | tf_op jit(solution)/shard_map/while/body/eval_jaxpr/dot_general | solution.py:22
  736.1 54.8 %all-reduce.9.cloned.1.call-done = f32[2560,64]{0,1:T(8,128)} async-done(((f32[2560,64]{0,1:T(8,128)}), f32[2560,64]{0,1:T(8,128)}) %all-reduce.9.cloned.1.call-update) | async-done | bytes 655376 | tf_op jit(solution)/shard_map/while/body/eval_jaxpr/psum | solution.py:13
  791.9 41.7 %all-reduce.11.cloned.1.call-done = f32[2560,64]{0,1:T(8,128)} async-done(((f32[2560,64]{0,1:T(8,128)}), f32[2560,64]{0,1:T(8,128)}) %all-reduce.11.cloned.1.call-update) | async-done | bytes 655376 | tf_op jit(solution)/shard_map/while/body/eval_jaxpr/psum | solution.py:9
  835.2 5.6 gather_fusion.1
  840.8 6.0 fusion.53
  846.9 29.3 %fusion.49 = f32[2560,64]{0,1:T(8,128)} fusion(f32[2,2560,2560]{2,1,0:T(8,128)} %get-tuple-element.329, s32[]{:T(128)S(6)} %select_n.295, f32[2560,64]{1,0:T(8,128)S(1)} %get-tuple-element.313, pred[]{:T(512)S(6)} %compare.37), kind=kOutput, calls=%fused_computation.4.clone.1 | convolution fusion | flops 5033328640 | bytes 27525124 | tf_op jit(solution)/shard_map/while/body/eval_jaxpr/dot_general | solution.py:22
  876.3 54.9 %all-reduce.5.cloned.1.call-done = f32[2560,64]{0,1:T(8,128)} async-done(((f32[2560,64]{0,1:T(8,128)}), f32[2560,64]{0,1:T(8,128)}) %all-reduce.5.cloned.1.call-update) | async-done | bytes 655376 | tf_op jit(solution)/shard_map/while/body/eval_jaxpr/psum | solution.py:13
  932.2 41.7 %all-reduce.7.cloned.1.call-done = f32[2560,64]{0,1:T(8,128)} async-done(((f32[2560,64]{0,1:T(8,128)}), f32[2560,64]{0,1:T(8,128)}) %all-reduce.7.cloned.1.call-update) | async-done | bytes 655376 | tf_op jit(solution)/shard_map/while/body/eval_jaxpr/psum | solution.py:9
  975.3 5.6 gather_fusion
  981.0 31.5 %fusion.51 = f32[2560,64]{0,1:T(8,128)} fusion(f32[2,2560,2560]{2,1,0:T(8,128)} %get-tuple-element.329, s32[]{:T(128)S(6)} %select_n.293, f32[2560,64]{1,0:T(8,128)} %get-tuple-element.330, f32[2560,64]{1,0:T(8,128)} %gather_fusion, f32[2560,64]{1,0:T(8,128)S(1)} %get-tuple-element.313, pred[2560]{0:T(1024)(128)(4,1)S(1)} %get-tuple-element.293, ...), kind=kOutput, calls=%fused_computation.6.clone.1 | convolution fusion | flops 5033820160 | bytes 30151684 | tf_op jit(solution)/shard_map/while/body/eval_jaxpr/dot_general | solution.py:22
  1012.6 54.8 %all-reduce.9.cloned.1.call-done = f32[2560,64]{0,1:T(8,128)} async-done(((f32[2560,64]{0,1:T(8,128)}), f32[2560,64]{0,1:T(8,128)}) %all-reduce.9.cloned.1.call-update) | async-done | bytes 655376 | tf_op jit(solution)/shard_map/while/body/eval_jaxpr/psum | solution.py:13
  1067.4 2.0 broadcast_select_fusion.6
  1069.5 40.6 %all-reduce.11.cloned.1.call-done = f32[2560,64]{0,1:T(8,128)} async-done(((f32[2560,64]{0,1:T(8,128)}), f32[2560,64]{0,1:T(8,128)}) %all-reduce.11.cloned.1.call-update) | async-done | bytes 655376 | tf_op jit(solution)/shard_map/while/body/eval_jaxpr/psum | solution.py:9
  1111.6 5.6 gather_fusion.1
  1117.2 6.0 fusion.53
  1123.2 11.0 gather_fusion.2
  1134.2 1.6 copy.19
  1135.8 2.3 broadcast_select_fusion.2
  1138.1 3.7 all-to-all-start.1
  1143.0 14.2 %all-to-all-done.1 = f32[8,512,64]{1,2,0:T(8,128)S(1)} async-done(((f32[8,512,64]{1,2,0:T(8,128)}), f32[8,512,64]{1,2,0:T(8,128)S(1)}, u32[]{:S(2)}, u32[]{:S(2)}) %all-to-all-start.1) | async-done | bytes 1048608 | tf_op jit(solution)/shard_map/all_to_all | solution.py:53
  1157.2 20.2 %fusion.32 = f32[1,1024,64]{1,2,0:T(8,128)} fusion(f32[1,1024,64]{1,2,0:T(8,128)S(1)} %copy-done, f32[4096,64]{0,1:T(8,128)S(1)} %bitcast.38, f32[1,1024,4096]{2,1,0:T(8,128)} %param.11), kind=kOutput, calls=%fused_computation.42 | convolution fusion | flops 3221291008 | bytes 18350080 | tf_op jit(solution)/shard_map/dot_general | solution.py:54
  (78 shorter events, 19.7 us)
Async XLA Ops:
  7.2 10.0 all-to-all-start
  17.2 84.4 %all-reduce.5.cloned.1.call-start = ((), (), s32[]{:S(2)}) async-start(), calls=%async_computation.2 | async-start | bytes 1310720 | tf_op jit(solution)/shard_map/while/body/eval_jaxpr/psum | solution.py:13
  46.6 97.8 %all-reduce.7.cloned.1.call-start = ((), (), s32[]{:S(2)}) async-start(), calls=%async_computation.3 | async-start | bytes 1310720 | tf_op jit(solution)/shard_map/while/body/eval_jaxpr/psum | solution.py:9
  102.5 135.5 %all-reduce.9.cloned.1.call-start = ((), (), s32[]{:S(2)}) async-start(), calls=%async_computation.4 | async-start | bytes 1310720 | tf_op jit(solution)/shard_map/while/body/eval_jaxpr/psum | solution.py:13
  183.0 97.6 %all-reduce.11.cloned.1.call-start = ((), (), s32[]{:S(2)}) async-start(), calls=%async_computation.5 | async-start | bytes 1310720 | tf_op jit(solution)/shard_map/while/body/eval_jaxpr/psum | solution.py:9
  293.8 84.4 %all-reduce.5.cloned.1.call-start = ((), (), s32[]{:S(2)}) async-start(), calls=%async_computation.2 | async-start | bytes 1310720 | tf_op jit(solution)/shard_map/while/body/eval_jaxpr/psum | solution.py:13
  323.2 97.6 %all-reduce.7.cloned.1.call-start = ((), (), s32[]{:S(2)}) async-start(), calls=%async_computation.3 | async-start | bytes 1310720 | tf_op jit(solution)/shard_map/while/body/eval_jaxpr/psum | solution.py:9
  379.1 135.3 %all-reduce.9.cloned.1.call-start = ((), (), s32[]{:S(2)}) async-start(), calls=%async_computation.4 | async-start | bytes 1310720 | tf_op jit(solution)/shard_map/while/body/eval_jaxpr/psum | solution.py:13
  459.5 97.7 %all-reduce.11.cloned.1.call-start = ((), (), s32[]{:S(2)}) async-start(), calls=%async_computation.5 | async-start | bytes 1310720 | tf_op jit(solution)/shard_map/while/body/eval_jaxpr/psum | solution.py:9
  570.4 84.3 %all-reduce.5.cloned.1.call-start = ((), (), s32[]{:S(2)}) async-start(), calls=%async_computation.2 | async-start | bytes 1310720 | tf_op jit(solution)/shard_map/while/body/eval_jaxpr/psum | solution.py:13
  599.8 97.6 %all-reduce.7.cloned.1.call-start = ((), (), s32[]{:S(2)}) async-start(), calls=%async_computation.3 | async-start | bytes 1310720 | tf_op jit(solution)/shard_map/while/body/eval_jaxpr/psum | solution.py:9
  655.6 135.3 %all-reduce.9.cloned.1.call-start = ((), (), s32[]{:S(2)}) async-start(), calls=%async_computation.4 | async-start | bytes 1310720 | tf_op jit(solution)/shard_map/while/body/eval_jaxpr/psum | solution.py:13
  736.0 97.6 %all-reduce.11.cloned.1.call-start = ((), (), s32[]{:S(2)}) async-start(), calls=%async_computation.5 | async-start | bytes 1310720 | tf_op jit(solution)/shard_map/while/body/eval_jaxpr/psum | solution.py:9
  846.8 84.4 %all-reduce.5.cloned.1.call-start = ((), (), s32[]{:S(2)}) async-start(), calls=%async_computation.2 | async-start | bytes 1310720 | tf_op jit(solution)/shard_map/while/body/eval_jaxpr/psum | solution.py:13
  876.2 97.6 %all-reduce.7.cloned.1.call-start = ((), (), s32[]{:S(2)}) async-start(), calls=%async_computation.3 | async-start | bytes 1310720 | tf_op jit(solution)/shard_map/while/body/eval_jaxpr/psum | solution.py:9
  932.1 135.3 %all-reduce.9.cloned.1.call-start = ((), (), s32[]{:S(2)}) async-start(), calls=%async_computation.4 | async-start | bytes 1310720 | tf_op jit(solution)/shard_map/while/body/eval_jaxpr/psum | solution.py:13
  1012.5 97.6 %all-reduce.11.cloned.1.call-start = ((), (), s32[]{:S(2)}) async-start(), calls=%async_computation.5 | async-start | bytes 1310720 | tf_op jit(solution)/shard_map/while/body/eval_jaxpr/psum | solution.py:9
  1138.1 19.0 %all-to-all-start.1 = ((f32[8,512,64]{1,2,0:T(8,128)}), f32[8,512,64]{1,2,0:T(8,128)S(1)}, u32[]{:S(2)}, u32[]{:S(2)}) async-start(f32[8,512,64]{1,2,0:T(8,128)} %broadcast_select_fusion.2), calls=%async_computation.1 | async-start | bytes 2097152 | tf_op jit(solution)/shard_map/all_to_all | solution.py:53
  1143.0 14.2 %copy-start = (f32[1,1024,64]{1,2,0:T(8,128)S(1)}, f32[1,1024,64]{1,2,0:T(8,128)}, u32[]{:S(2)}) copy-start(f32[1,1024,64]{1,2,0:T(8,128)} %param.12) | copy-start | bytes 786436
Sparse Core Ops, SparseCore 0:
  46.7 54.7 all-reduce.4
  104.5 39.8 all-reduce.6
  183.2 54.7 all-reduce.8
  240.7 39.8 all-reduce.10
  323.3 54.7 all-reduce.4
  380.9 39.8 all-reduce.6
  459.6 54.7 all-reduce.8
  517.3 39.8 all-reduce.10
  599.9 54.7 all-reduce.4
  657.5 39.8 all-reduce.6
  736.2 54.7 all-reduce.8
  793.8 39.8 all-reduce.10
  876.3 54.7 all-reduce.4
  933.9 39.8 all-reduce.6
  1012.6 54.7 all-reduce.8
  1070.2 39.8 all-reduce.10
where the time goes:
time: 1190 us; the launch traced here: 1180 us
  waiting for transfers between devices  787 us (66%)
  matrix products  264 us (22%)
  local copies, waits for them, and re-layouts  73.1 us (6%)
  other arithmetic  36 us (3%)
  between operations  13.7 us (1%)
    psum x8, waiting for transfers between devices, spread_panel(): summed = lax.psum(partial_value, 'col')  439 us
    psum x8, waiting for transfers between devices, spread(): return lax.psum(block, axis)  332 us
    dot_general x8, matrix products, solve_panel(): jnp.dot(panel_rows, solved, precision=lax.Precision.HIGHEST, preferred_el...  243 us
    gather x8, local copies, waits for them, and re-layouts, solve_panel(): picked = jnp.take(summed, jnp.clip(offset, 0, panel_size - 1), axis=0)  44.9 us
    select_n x4, other arithmetic, solve_panel(): return jnp.where(inside[:, None], root_rhs - picked, solved)  24 us
  transfers between devices with their start and end apart: 18, of which 18 were waited for; matrix products, arithmetic and copies ran while one was open for 0% of the time, Pallas kernels for 0%

commit v1 on v0

--- a/solution.py
+++ b/solution.py
@@ -10,7 +10,7 @@
 
 
 def spread_panel(partial_value, owner_row):
-    summed = lax.psum(partial_value, "col")
+    summed = jnp.sum(lax.all_gather(partial_value, "col"), axis=0)
     return spread(summed, "row", owner_row)
 
 

time: 1190 us -> 1280 us (1.076)
  local copies, waits for them, and re-layouts: 73.1 us -> 117 us
  waiting for transfers between devices: 787 us -> 821 us
  other arithmetic: 36 us -> 49.1 us
    psum x8 -> x0, waiting for transfers between devices: 439 us -> none  [spread_panel(): summed = lax.psum(partial_value, 'col')]
    all_gather x0 -> x8, waiting for transfers between devices: none -> 325 us  [spread_panel(): summed = jnp.sum(lax.all_gather(partial_value, 'col'), axis=0)]
    psum x8, waiting for transfers between devices: 332 us -> 479 us  [spread(): return lax.psum(block, axis)]
    while x0 -> x8, local copies, waits for them, and re-layouts: none -> 43.6 us
where the time goes in v1:
time: 1280 us
  waiting for transfers between devices  821 us (64%)
  matrix products  267 us (21%)
  local copies, waits for them, and re-layouts  117 us (9%)
  other arithmetic  49.1 us (4%)
  between operations  13.8 us (1%)
    psum x8, waiting for transfers between devices, spread(): return lax.psum(block, axis)  479 us
    all_gather x8, waiting for transfers between devices, spread_panel(): summed = jnp.sum(lax.all_gather(partial_value, 'col'), axis=0)  325 us
    dot_general x8, matrix products, solve_panel(): jnp.dot(panel_rows, solved, precision=lax.Precision.HIGHEST, preferred_el...  247 us
    gather x8, local copies, waits for them, and re-layouts, solve_panel(): picked = jnp.take(summed, jnp.clip(offset, 0, panel_size - 1), axis=0)  49.5 us
    while x8, local copies, waits for them, and re-layouts  43.6 us
  transfers between devices with their start and end apart: 18, of which 18 were waited for; matrix products, arithmetic and copies ran while one was open for 0% of the time, Pallas kernels for 0%

profile of v1, /device:TPU:0, one launch (start us, length us, event | category | flops | bytes accessed | tf_op | source)
XLA Modules:
  0.0 1278.1 jit_solution(2389579704801774783)
XLA Ops:
  18.4 1199.2 %while.19 = (s32[]{:T(128)}, f32[2560,64]{1,0:T(8,128)S(1)}, f32[2,2560,2560]{2,1,0:T(8,128)}, f32[2560,64]{1,0:T(8,128)}, s32[]{:T(128)}, /*index=5*/s32[]{:T(1...) while((s32[]{:T(128)}, f32[2560,64]{1,0:T(8,128)S(1)}, ...), condition=%wide.region_5.7_spmd.clone, body=%wide.region_0.6_spmd.clone.sunk | while | flops 10071343104 | bytes 146913200 | solution.py:45
  18.4 29.3 %fusion.49 = f32[2560,64]{0,1:T(8,128)} fusion(f32[2,2560,2560]{2,1,0:T(8,128)} %get-tuple-element.329, s32[]{:T(128)S(6)} %select_n.295, f32[2560,64]{1,0:T(8,128)S(1)} %get-tuple-element.313, pred[]{:T(512)S(6)} %compare.37), kind=kOutput, calls=%fused_computation.4.clone.1 | convolution fusion | flops 5033328640 | bytes 27525124 | tf_op jit(solution)/shard_map/while/body/eval_jaxpr/dot_general | solution.py:22
  47.8 40.6 %all-gather.11.cloned.1.call-done = f32[20480,64]{0,1:T(8,128)} async-done(((f32[2560,64]{0,1:T(8,128)}), f32[20480,64]{0,1:T(8,128)}) %all-gather.11.cloned.1.call-update) | async-done | bytes 5242896 | tf_op jit(solution)/shard_map/while/body/eval_jaxpr/all_gather | solution.py:13
  88.4 5.4 copy.31
  96.9 60.1 %all-reduce.3.cloned.1.call-done = f32[2560,64]{1,0:T(8,128)} async-done(((f32[2560,64]{1,0:T(8,128)}), f32[2560,64]{1,0:T(8,128)}) %all-reduce.3.cloned.1.call-update) | async-done | bytes 655376 | tf_op jit(solution)/shard_map/while/body/eval_jaxpr/psum | solution.py:9
  157.0 5.5 gather_fusion
  162.5 32.3 %fusion.51 = f32[2560,64]{0,1:T(8,128)} fusion(f32[2,2560,2560]{2,1,0:T(8,128)} %get-tuple-element.329, s32[]{:T(128)S(6)} %select_n.293, f32[2560,64]{1,0:T(8,128)} %get-tuple-element.330, f32[2560,64]{1,0:T(8,128)S(1)} %gather_fusion, f32[2560,64]{1,0:T(8,128)S(1)} %get-tuple-element.313, pred[2560]{0:T(1024)(128)(4,1)S(1)} %get-tuple-element.293, ...), kind=kOutput, calls=%fused_computation.6.clone.1 | convolution fusion | flops 5033820160 | bytes 29496324 | tf_op jit(solution)/shard_map/while/body/eval_jaxpr/dot_general | solution.py:22
  194.9 40.6 %all-gather.13.cloned.1.call-done = f32[20480,64]{0,1:T(8,128)} async-done(((f32[2560,64]{0,1:T(8,128)}), f32[20480,64]{0,1:T(8,128)}) %all-gather.13.cloned.1.call-update) | async-done | bytes 5242896 | tf_op jit(solution)/shard_map/while/body/eval_jaxpr/all_gather | solution.py:13
  235.5 5.4 copy.33
  245.0 60.6 %all-reduce.5.cloned.1.call-done = f32[2560,64]{1,0:T(8,128)} async-done(((f32[2560,64]{1,0:T(8,128)}), f32[2560,64]{1,0:T(8,128)}) %all-reduce.5.cloned.1.call-update) | async-done | bytes 655376 | tf_op jit(solution)/shard_map/while/body/eval_jaxpr/psum | solution.py:9
  305.5 6.9 gather_fusion.1
  312.5 5.7 fusion.53
  318.3 29.3 %fusion.49 = f32[2560,64]{0,1:T(8,128)} fusion(f32[2,2560,2560]{2,1,0:T(8,128)} %get-tuple-element.329, s32[]{:T(128)S(6)} %select_n.295, f32[2560,64]{1,0:T(8,128)S(1)} %get-tuple-element.313, pred[]{:T(512)S(6)} %compare.37), kind=kOutput, calls=%fused_computation.4.clone.1 | convolution fusion | flops 5033328640 | bytes 27525124 | tf_op jit(solution)/shard_map/while/body/eval_jaxpr/dot_general | solution.py:22
  347.7 40.6 %all-gather.11.cloned.1.call-done = f32[20480,64]{0,1:T(8,128)} async-done(((f32[2560,64]{0,1:T(8,128)}), f32[20480,64]{0,1:T(8,128)}) %all-gather.11.cloned.1.call-update) | async-done | bytes 5242896 | tf_op jit(solution)/shard_map/while/body/eval_jaxpr/all_gather | solution.py:13
  388.3 5.4 copy.31
  396.8 60.1 %all-reduce.3.cloned.1.call-done = f32[2560,64]{1,0:T(8,128)} async-done(((f32[2560,64]{1,0:T(8,128)}), f32[2560,64]{1,0:T(8,128)}) %all-reduce.3.cloned.1.call-update) | async-done | bytes 655376 | tf_op jit(solution)/shard_map/while/body/eval_jaxpr/psum | solution.py:9
  456.9 5.5 gather_fusion
  462.4 32.3 %fusion.51 = f32[2560,64]{0,1:T(8,128)} fusion(f32[2,2560,2560]{2,1,0:T(8,128)} %get-tuple-element.329, s32[]{:T(128)S(6)} %select_n.293, f32[2560,64]{1,0:T(8,128)} %get-tuple-element.330, f32[2560,64]{1,0:T(8,128)S(1)} %gather_fusion, f32[2560,64]{1,0:T(8,128)S(1)} %get-tuple-element.313, pred[2560]{0:T(1024)(128)(4,1)S(1)} %get-tuple-element.293, ...), kind=kOutput, calls=%fused_computation.6.clone.1 | convolution fusion | flops 5033820160 | bytes 29496324 | tf_op jit(solution)/shard_map/while/body/eval_jaxpr/dot_general | solution.py:22
  494.8 40.6 %all-gather.13.cloned.1.call-done = f32[20480,64]{0,1:T(8,128)} async-done(((f32[2560,64]{0,1:T(8,128)}), f32[20480,64]{0,1:T(8,128)}) %all-gather.13.cloned.1.call-update) | async-done | bytes 5242896 | tf_op jit(solution)/shard_map/while/body/eval_jaxpr/all_gather | solution.py:13
  535.4 5.4 copy.33
  546.2 58.9 %all-reduce.5.cloned.1.call-done = f32[2560,64]{1,0:T(8,128)} async-done(((f32[2560,64]{1,0:T(8,128)}), f32[2560,64]{1,0:T(8,128)}) %all-reduce.5.cloned.1.call-update) | async-done | bytes 655376 | tf_op jit(solution)/shard_map/while/body/eval_jaxpr/psum | solution.py:9
  605.1 6.9 gather_fusion.1
  612.0 5.7 fusion.53
  617.8 29.3 %fusion.49 = f32[2560,64]{0,1:T(8,128)} fusion(f32[2,2560,2560]{2,1,0:T(8,128)} %get-tuple-element.329, s32[]{:T(128)S(6)} %select_n.295, f32[2560,64]{1,0:T(8,128)S(1)} %get-tuple-element.313, pred[]{:T(512)S(6)} %compare.37), kind=kOutput, calls=%fused_computation.4.clone.1 | convolution fusion | flops 5033328640 | bytes 27525124 | tf_op jit(solution)/shard_map/while/body/eval_jaxpr/dot_general | solution.py:22
  647.2 40.6 %all-gather.11.cloned.1.call-done = f32[20480,64]{0,1:T(8,128)} async-done(((f32[2560,64]{0,1:T(8,128)}), f32[20480,64]{0,1:T(8,128)}) %all-gather.11.cloned.1.call-update) | async-done | bytes 5242896 | tf_op jit(solution)/shard_map/while/body/eval_jaxpr/all_gather | solution.py:13
  687.8 5.4 copy.31
  696.3 60.1 %all-reduce.3.cloned.1.call-done = f32[2560,64]{1,0:T(8,128)} async-done(((f32[2560,64]{1,0:T(8,128)}), f32[2560,64]{1,0:T(8,128)}) %all-reduce.3.cloned.1.call-update) | async-done | bytes 655376 | tf_op jit(solution)/shard_map/while/body/eval_jaxpr/psum | solution.py:9
  756.4 5.5 gather_fusion
  761.9 32.4 %fusion.51 = f32[2560,64]{0,1:T(8,128)} fusion(f32[2,2560,2560]{2,1,0:T(8,128)} %get-tuple-element.329, s32[]{:T(128)S(6)} %select_n.293, f32[2560,64]{1,0:T(8,128)} %get-tuple-element.330, f32[2560,64]{1,0:T(8,128)S(1)} %gather_fusion, f32[2560,64]{1,0:T(8,128)S(1)} %get-tuple-element.313, pred[2560]{0:T(1024)(128)(4,1)S(1)} %get-tuple-element.293, ...), kind=kOutput, calls=%fused_computation.6.clone.1 | convolution fusion | flops 5033820160 | bytes 29496324 | tf_op jit(solution)/shard_map/while/body/eval_jaxpr/dot_general | solution.py:22
  794.4 40.6 %all-gather.13.cloned.1.call-done = f32[20480,64]{0,1:T(8,128)} async-done(((f32[2560,64]{0,1:T(8,128)}), f32[20480,64]{0,1:T(8,128)}) %all-gather.13.cloned.1.call-update) | async-done | bytes 5242896 | tf_op jit(solution)/shard_map/while/body/eval_jaxpr/all_gather | solution.py:13
  835.1 5.4 copy.33
  844.5 60.6 %all-reduce.5.cloned.1.call-done = f32[2560,64]{1,0:T(8,128)} async-done(((f32[2560,64]{1,0:T(8,128)}), f32[2560,64]{1,0:T(8,128)}) %all-reduce.5.cloned.1.call-update) | async-done | bytes 655376 | tf_op jit(solution)/shard_map/while/body/eval_jaxpr/psum | solution.py:9
  905.1 6.9 gather_fusion.1
  912.0 5.7 fusion.53
  917.8 29.3 %fusion.49 = f32[2560,64]{0,1:T(8,128)} fusion(f32[2,2560,2560]{2,1,0:T(8,128)} %get-tuple-element.329, s32[]{:T(128)S(6)} %select_n.295, f32[2560,64]{1,0:T(8,128)S(1)} %get-tuple-element.313, pred[]{:T(512)S(6)} %compare.37), kind=kOutput, calls=%fused_computation.4.clone.1 | convolution fusion | flops 5033328640 | bytes 27525124 | tf_op jit(solution)/shard_map/while/body/eval_jaxpr/dot_general | solution.py:22
  947.2 40.6 %all-gather.11.cloned.1.call-done = f32[20480,64]{0,1:T(8,128)} async-done(((f32[2560,64]{0,1:T(8,128)}), f32[20480,64]{0,1:T(8,128)}) %all-gather.11.cloned.1.call-update) | async-done | bytes 5242896 | tf_op jit(solution)/shard_map/while/body/eval_jaxpr/all_gather | solution.py:13
  987.9 5.4 copy.31
  996.4 60.1 %all-reduce.3.cloned.1.call-done = f32[2560,64]{1,0:T(8,128)} async-done(((f32[2560,64]{1,0:T(8,128)}), f32[2560,64]{1,0:T(8,128)}) %all-reduce.3.cloned.1.call-update) | async-done | bytes 655376 | tf_op jit(solution)/shard_map/while/body/eval_jaxpr/psum | solution.py:9
  1056.5 5.5 gather_fusion
  1061.9 32.4 %fusion.51 = f32[2560,64]{0,1:T(8,128)} fusion(f32[2,2560,2560]{2,1,0:T(8,128)} %get-tuple-element.329, s32[]{:T(128)S(6)} %select_n.293, f32[2560,64]{1,0:T(8,128)} %get-tuple-element.330, f32[2560,64]{1,0:T(8,128)S(1)} %gather_fusion, f32[2560,64]{1,0:T(8,128)S(1)} %get-tuple-element.313, pred[2560]{0:T(1024)(128)(4,1)S(1)} %get-tuple-element.293, ...), kind=kOutput, calls=%fused_computation.6.clone.1 | convolution fusion | flops 5033820160 | bytes 29496324 | tf_op jit(solution)/shard_map/while/body/eval_jaxpr/dot_general | solution.py:22
  1094.4 40.6 %all-gather.13.cloned.1.call-done = f32[20480,64]{0,1:T(8,128)} async-done(((f32[2560,64]{0,1:T(8,128)}), f32[20480,64]{0,1:T(8,128)}) %all-gather.13.cloned.1.call-update) | async-done | bytes 5242896 | tf_op jit(solution)/shard_map/while/body/eval_jaxpr/all_gather | solution.py:13
  1135.1 5.4 copy.33
  1145.9 58.9 %all-reduce.5.cloned.1.call-done = f32[2560,64]{1,0:T(8,128)} async-done(((f32[2560,64]{1,0:T(8,128)}), f32[2560,64]{1,0:T(8,128)}) %all-reduce.5.cloned.1.call-update) | async-done | bytes 655376 | tf_op jit(solution)/shard_map/while/body/eval_jaxpr/psum | solution.py:9
  1204.7 6.9 gather_fusion.1
  1211.6 5.7 fusion.53
  1217.6 10.8 gather_fusion.2
  1237.2 14.2 %all-to-all-done.1 = f32[8,512,64]{1,2,0:T(8,128)S(1)} async-done(((f32[8,512,64]{1,2,0:T(8,128)}), f32[8,512,64]{1,2,0:T(8,128)S(1)}, u32[]{:S(2)}, u32[]{:S(2)}) %all-to-all-start.1) | async-done | bytes 1048608 | tf_op jit(solution)/shard_map/all_to_all | solution.py:53
  1251.4 20.2 %fusion.32 = f32[1,1024,64]{1,2,0:T(8,128)} fusion(f32[1,1024,64]{1,2,0:T(8,128)S(1)} %copy-done, f32[4096,64]{0,1:T(8,128)S(1)} %bitcast.58, f32[1,1024,4096]{2,1,0:T(8,128)} %param.11), kind=kOutput, calls=%fused_computation.44 | convolution fusion | flops 3221291008 | bytes 18350080 | tf_op jit(solution)/shard_map/dot_general | solution.py:54
  (98 shorter events, 51.1 us)
Async XLA Ops:
  7.2 10.0 all-to-all-start
  18.4 1199.2 %copy-start.2 = (s32[4096]{0:T(1024)S(1)}, s32[4096]{0:T(1024)}, u32[]{:S(2)}) copy-start(s32[4096]{0:T(1024)} %broadcast_clamp_fusion) | copy-start | bytes 49156
  18.4 70.1 %all-gather.11.cloned.1.call-start = ((), (), s32[]{:S(2)}) async-start(), calls=%async_computation.2 | async-start | bytes 5898240 | tf_op jit(solution)/shard_map/while/body/eval_jaxpr/all_gather | solution.py:13
  47.7 109.3 %all-reduce.3.cloned.1.call-start = ((), (), s32[]{:S(2)}) async-start(), calls=%async_computation.3 | async-start | bytes 2621440 | tf_op jit(solution)/shard_map/while/body/eval_jaxpr/psum | solution.py:9
  96.8 138.7 %all-gather.13.cloned.1.call-start = ((), (), s32[]{:S(2)}) async-start(), calls=%async_computation.4 | async-start | bytes 5898240 | tf_op jit(solution)/shard_map/while/body/eval_jaxpr/all_gather | solution.py:13
  194.8 110.7 %all-reduce.5.cloned.1.call-start = ((), (), s32[]{:S(2)}) async-start(), calls=%async_computation.5 | async-start | bytes 2621440 | tf_op jit(solution)/shard_map/while/body/eval_jaxpr/psum | solution.py:9
  318.2 70.1 %all-gather.11.cloned.1.call-start = ((), (), s32[]{:S(2)}) async-start(), calls=%async_computation.2 | async-start | bytes 5898240 | tf_op jit(solution)/shard_map/while/body/eval_jaxpr/all_gather | solution.py:13
  347.6 109.3 %all-reduce.3.cloned.1.call-start = ((), (), s32[]{:S(2)}) async-start(), calls=%async_computation.3 | async-start | bytes 2621440 | tf_op jit(solution)/shard_map/while/body/eval_jaxpr/psum | solution.py:9
  396.7 138.7 %all-gather.13.cloned.1.call-start = ((), (), s32[]{:S(2)}) async-start(), calls=%async_computation.4 | async-start | bytes 5898240 | tf_op jit(solution)/shard_map/while/body/eval_jaxpr/all_gather | solution.py:13
  494.7 110.3 %all-reduce.5.cloned.1.call-start = ((), (), s32[]{:S(2)}) async-start(), calls=%async_computation.5 | async-start | bytes 2621440 | tf_op jit(solution)/shard_map/while/body/eval_jaxpr/psum | solution.py:9
  617.7 70.1 %all-gather.11.cloned.1.call-start = ((), (), s32[]{:S(2)}) async-start(), calls=%async_computation.2 | async-start | bytes 5898240 | tf_op jit(solution)/shard_map/while/body/eval_jaxpr/all_gather | solution.py:13
  647.1 109.3 %all-reduce.3.cloned.1.call-start = ((), (), s32[]{:S(2)}) async-start(), calls=%async_computation.3 | async-start | bytes 2621440 | tf_op jit(solution)/shard_map/while/body/eval_jaxpr/psum | solution.py:9
  696.2 138.9 %all-gather.13.cloned.1.call-start = ((), (), s32[]{:S(2)}) async-start(), calls=%async_computation.4 | async-start | bytes 5898240 | tf_op jit(solution)/shard_map/while/body/eval_jaxpr/all_gather | solution.py:13
  794.4 110.7 %all-reduce.5.cloned.1.call-start = ((), (), s32[]{:S(2)}) async-start(), calls=%async_computation.5 | async-start | bytes 2621440 | tf_op jit(solution)/shard_map/while/body/eval_jaxpr/psum | solution.py:9
  917.7 70.1 %all-gather.11.cloned.1.call-start = ((), (), s32[]{:S(2)}) async-start(), calls=%async_computation.2 | async-start | bytes 5898240 | tf_op jit(solution)/shard_map/while/body/eval_jaxpr/all_gather | solution.py:13
  947.2 109.3 %all-reduce.3.cloned.1.call-start = ((), (), s32[]{:S(2)}) async-start(), calls=%async_computation.3 | async-start | bytes 2621440 | tf_op jit(solution)/shard_map/while/body/eval_jaxpr/psum | solution.py:9
  996.2 138.9 %all-gather.13.cloned.1.call-start = ((), (), s32[]{:S(2)}) async-start(), calls=%async_computation.4 | async-start | bytes 5898240 | tf_op jit(solution)/shard_map/while/body/eval_jaxpr/all_gather | solution.py:13
  1094.4 110.3 %all-reduce.5.cloned.1.call-start = ((), (), s32[]{:S(2)}) async-start(), calls=%async_computation.5 | async-start | bytes 2621440 | tf_op jit(solution)/shard_map/while/body/eval_jaxpr/psum | solution.py:9
  1228.3 1.6 copy-start.1
  1232.3 19.0 %all-to-all-start.1 = ((f32[8,512,64]{1,2,0:T(8,128)}), f32[8,512,64]{1,2,0:T(8,128)S(1)}, u32[]{:S(2)}, u32[]{:S(2)}) async-start(f32[8,512,64]{1,2,0:T(8,128)} %broadcast_select_fusion.2), calls=%async_computation.1 | async-start | bytes 2097152 | tf_op jit(solution)/shard_map/all_to_all | solution.py:53
  1237.2 14.2 %copy-start = (f32[1,1024,64]{1,2,0:T(8,128)S(1)}, f32[1,1024,64]{1,2,0:T(8,128)}, u32[]{:S(2)}) copy-start(f32[1,1024,64]{1,2,0:T(8,128)} %param.12) | copy-start | bytes 786436
Sparse Core Ops, SparseCore 0:
  47.8 40.5 all-gather.10
  96.9 60.0 all-reduce.2
  194.9 40.5 all-gather.12
  245.0 60.4 all-reduce.4
  347.7 40.5 all-gather.10
  396.8 60.0 all-reduce.2
  494.8 40.5 all-gather.12
  546.3 58.7 all-reduce.4
  647.3 40.5 all-gather.10
  696.3 60.0 all-reduce.2
  794.5 40.5 all-gather.12
  844.6 60.4 all-reduce.4
  947.3 40.5 all-gather.10
  996.3 60.0 all-reduce.2
  1094.5 40.5 all-gather.12
  1145.9 58.7 all-reduce.4
